TPU v7x, 32 devices: a whole 2x2x4 slice. The times are simulated.
32 devices in a mesh: shot: 16 (over z, y, core), surf: 2 (over x).
Axes of the slice: x: 2, y: 2, z: 4, core: 2. Of those that a mesh axis runs over, the one named last changes fastest.
Arguments:
- data: float32 [32, 256, 512], P('shot', 'surf'), may hold values from -6 to 6
- positions: int32 [256], P('surf'), may hold values from 0 to 63, as said below
- plan: int32 [16], replicated, may hold values from 0 to 15, each once
- primaries: bfloat16 [64, 16, 16, 256], P('surf', None, 'shot'), may hold values from -0.03125 to 0.03125
- scale: float32 [32], P('shot'), may hold values from 0.5 to 1.5
Outputs:
- demultiplied: float32 [32, 256, 512], P('shot', 'surf')
Inputs may be any that keep to these rules, and one draw needn't show every extreme that they name: `positions`: receiver r lies at a position of the block [b * 32, (b + 1) * 32) with b = r // 128; in each such block of receivers the first maps to the block's first position and the last to its last. A permutation: slot i of primaries holds receiver panel plan[i].
All inputs are finite; a program needn't handle non-finite values.
Results may differ from a plain program's by a relative error of at most 0.0065.
Values may be sent and summed in bfloat16 or wider, within the bound.
A program may use at most 128 MiB of HBM per device.

v0:
```python
import math

import jax
import jax.numpy as jnp
from jax import lax
from jax.sharding import PartitionSpec as P


def fourier_matrices(samples):
    length = 2 * samples
    time_index = jnp.arange(samples, dtype=jnp.int32)
    phase_index = time_index[:, None] * time_index[None, :] % length
    angles = phase_index.astype(jnp.float32) * (2.0 * math.pi / length)
    cosine = jnp.cos(angles)
    sine_part = jnp.sin(angles)
    alternate = (1 - 2 * (time_index % 2)).astype(jnp.float32)
    nyquist = time_index == 0
    forward_imag = jnp.where(nyquist[None, :], alternate[:, None], -sine_part)
    forward = jnp.concatenate([cosine, forward_imag], axis=1).astype(jnp.bfloat16)
    weights = jnp.where(nyquist, 1.0, 2.0).astype(jnp.float32) / length
    backward_real_table = cosine.T * weights[:, None]
    inverse_imag = jnp.where(
        nyquist[:, None], alternate[None, :] / length, -2.0 * sine_part.T / length
    )
    inverse = jnp.concatenate([backward_real_table, inverse_imag], axis=0).astype(jnp.bfloat16)
    return (forward, inverse)


def spectral_product(left, right):
    half = left.shape[-1] // 2
    left_real = left[..., :half]
    left_imag = left[..., half:]
    right_real = right[..., :half]
    right_imag = right[..., half:]

    def contract(leading_factor, trailing_factor):
        return jnp.einsum(
            "quw,ugw->qgw", leading_factor, trailing_factor, preferred_element_type=jnp.float32
        )

    real_cross_term = contract(left_real, right_real)
    imaginary_cross_term = contract(left_imag, right_imag)
    crossed = contract(left_real, right_imag) + contract(left_imag, right_real)
    interior = (jnp.arange(half) > 0).astype(jnp.float32)
    return jnp.concatenate(
        [
            real_cross_term - interior * imaginary_cross_term,
            interior * crossed + (1.0 - interior) * imaginary_cross_term,
        ],
        axis=-1,
    )


def on_device(data, positions, plan, primaries, scale):
    shot_count, receiver_count, samples = data.shape
    position_count = primaries.shape[0]
    panel_width = primaries.shape[1]
    tap_count = primaries.shape[3]
    panel_total = plan.shape[0]
    forward, inverse = fourier_matrices(samples)
    local_index = positions - lax.axis_index("surf") * position_count
    onehot = (local_index[:, None] == jnp.arange(position_count, dtype=jnp.int32)[None, :]).astype(
        jnp.float32
    )
    gathered = jnp.einsum("srt,rx->sxt", data, onehot, precision=lax.Precision.HIGHEST).astype(
        jnp.bfloat16
    )
    panel_order = jnp.argsort(plan)
    data_spectra = jnp.dot(
        gathered.reshape(-1, samples), forward, preferred_element_type=jnp.float32
    )
    data_spectra = data_spectra.astype(jnp.bfloat16).reshape(
        shot_count, position_count, 2 * samples
    )
    piece_rows = lax.all_gather(primaries, "shot", axis=2, tiled=True)
    piece_count = piece_rows.shape[2]
    spectrum = jnp.dot(
        piece_rows.reshape(-1, tap_count), forward[:tap_count], preferred_element_type=jnp.float32
    )
    spectrum = spectrum.astype(jnp.bfloat16).reshape(
        position_count, panel_width * piece_count, 2 * samples
    )
    product = spectral_product(data_spectra, spectrum)
    partial_value = product.reshape(shot_count, panel_width, piece_count, 2 * samples)
    summed = lax.psum_scatter(
        partial_value.astype(jnp.bfloat16), "surf", scatter_dimension=1, tiled=True
    ).astype(jnp.float32)
    rows_kept = summed.shape[1]
    spectrum = summed.astype(jnp.bfloat16)
    arrived = jnp.dot(
        spectrum.reshape(-1, 2 * samples), inverse, preferred_element_type=jnp.float32
    )
    arrived = arrived.reshape(shot_count, rows_kept, panel_total, samples)
    ordered = jnp.take(arrived, panel_order, axis=2)
    prediction = ordered.reshape(shot_count, receiver_count, samples)
    return data - scale[:, None, None] * prediction


def solution(mesh):
    in_specs = (P("shot", "surf", None), P("surf"), P(), P("surf", None, "shot", None), P("shot"))
    out_specs = P("shot", "surf", None)
    return jax.shard_map(
        on_device, mesh=mesh, in_specs=in_specs, out_specs=out_specs, check_vma=False
    )
```

profile of v0, /device:TPU:0, one launch (start us, length us, event | category | flops | bytes accessed | tf_op | source)
XLA Modules:
  0.0 134.5 jit_solution(13501440312715912721)
XLA Ops:
  6.5 0.0 all-gather.2.cloned.1.call-start
  6.5 0.7 all-gather.2.cloned.1.call-update
  7.3 0.0 reduce-scatter.5.cloned.1.call-start
  7.3 3.9 %fusion.26 = bf16[512,512]{1,0:T(8,128)(2,1)S(1)} fusion(), kind=kLoop, calls=%fused_computation.41 | loop fusion | flops 3932160 | bytes 524288 | tf_op jit(solution)/shard_map/convert.6
  11.3 0.7 broadcast_subtract_fusion.1
  11.9 1.3 convolution_convert_fusion.2
  13.3 5.0 %select_convert_fusion.1 = (bf16[512,512]{1,0:T(8,128)(2,1)S(1)}, bf16[512,512]{1,0:T(8,128)(2,1)}) fusion(bf16[512]{0:T(512)(128)(2,1)S(1)} %fusion.32, pred[512]{0:T(512)(128)(4,1)S(1)} %iota_compare_fusion.2, bf16[512]{0:T(512)(128)(2,1)S(1)} %broadcast_multiply_fusion), kind=kLoop, calls=%fused_computation.28 | loop fusion | flops 4718592 | bytes 1051136 | tf_op jit(solution)/shard_map/convert.7
  18.3 0.3 convolution_convert_fusion.1
  18.6 0.2 copy.34
  18.8 0.0 copy-start.3
  18.8 0.9 copy.33
  19.7 0.6 fusion.36
  20.3 0.6 broadcast_subtract_fusion
  20.8 41.9 %all-gather.2.cloned.1.call-done = bf16[32,16,16,256]{3,1,0,2:T(8,128)(2,1)} async-done(((bf16[32,16,1,256]{3,1,0,2:T(8,128)(2,1)}), bf16[32,16,16,256]{3,1,0,2:T(8,128)(2,1)}) %all-gather.2.cloned.1.call-update) | async-done | bytes 4194320 | tf_op jit(solution)/shard_map/all_gather | solution.py:75
  62.8 5.6 %copy.21 = bf16[32,16,16,256]{3,2,1,0:T(8,128)(2,1)S(1)} copy(bf16[32,16,16,256]{3,1,0,2:T(8,128)(2,1)} %all-gather.2.cloned.1.call-done) | data formatting | bytes 8388608 | tf_op jit(solution)/shard_map/all_gather | solution.py:75
  68.4 8.1 %convolution_convert_fusion = bf16[1024,8192]{1,0:T(8,128)(2,1)} fusion(bf16[8192,256]{1,0:T(8,128)(2,1)S(1)} %bitcast.58, bf16[512,512]{1,0:T(8,128)(2,1)S(1)} %get-tuple-element.9, bf16[512,512]{1,0:T(8,128)(2,1)S(1)} %fusion.26), kind=kOutput, calls=%fused_computation.1 | convolution fusion | flops 4304404480 | bytes 22020096 | tf_op jit(solution)/shard_map/dot_general | solution.py:77
  76.5 10.4 %copy.35 = bf16[128,8,32,256]{3,2,1,0:T(8,128)(2,1)S(1)} copy(bf16[128,8,32,256]{3,1,2,0:T(8,128)(2,1)} %bitcast.57) | data formatting | bytes 33554432
  86.9 0.0 copy-done.3
  86.9 0.0 copy-start.4
  87.0 2.2 %fusion.41 = f32[512,256,2]{1,2,0:T(2,128)} fusion(bf16[32,256,1024]{1,0,2:T(8,128)(2,1)S(1)} %bitcast.53, bf16[2,32,512]{1,0,2:T(2,128)(2,1)S(1)} %copy.34), kind=kOutput, calls=%fused_computation.67 | convolution fusion | flops 16777216 | bytes 17891328 | tf_op jit(solution)/shard_map/quw,ugw->qgw/dot_general | solution.py:37
  89.2 0.0 copy-done.4
  89.2 0.0 copy-start
  89.2 0.0 copy-start.2
  89.2 2.2 %fusion.42 = f32[512,256,2]{1,2,0:T(2,128)} fusion(bf16[32,256,1024]{1,0,2:T(8,128)(2,1)S(1)} %bitcast.54, bf16[2,32,512]{1,0,2:T(2,128)(2,1)S(1)} %copy-done.4), kind=kOutput, calls=%fused_computation.68 | convolution fusion | flops 16777216 | bytes 17891328 | tf_op jit(solution)/shard_map/quw,ugw->qgw/dot_general | solution.py:37
  91.4 0.0 copy-done
  91.4 0.0 copy-done.2
  91.4 0.0 copy-start.1
  91.4 2.0 %fusion.5 = bf16[2,256,512]{1,0,2:T(2,128)(2,1)} fusion(bf16[32,256,1024]{1,0,2:T(8,128)(2,1)S(1)} %bitcast.55, bf16[2,32,512]{1,0,2:T(2,128)(2,1)S(1)} %copy-done.4, f32[512,256,2]{1,2,0:T(2,128)S(1)} %copy-done.2, f32[512]{0:T(512)S(1)} %copy-done), kind=kOutput, calls=%fused_computation.12 | convolution fusion | flops 17563648 | bytes 18417664 | tf_op jit(solution)/shard_map/quw,ugw->qgw/dot_general | solution.py:37
  93.4 0.0 copy-done.1
  93.4 0.0 copy-start.5
  93.4 3.7 %fusion.4 = bf16[2,256,512]{1,0,2:T(2,128)(2,1)} fusion(f32[512,256,2]{1,2,0:T(2,128)} %fusion.42, bf16[32,256,1024]{1,0,2:T(8,128)(2,1)S(1)} %bitcast.56, bf16[2,32,512]{1,0,2:T(2,128)(2,1)} %copy-done.3, f32[512,256,2]{1,2,0:T(2,128)S(1)} %copy-done.2, f32[512]{0:T(512)S(1)} %copy-done.1, f32[512]{0:T(512)S(1)} %copy-done), kind=kOutput, calls=%fused_computation.11 | convolution fusion | flops 18087936 | bytes 19468288 | tf_op jit(solution)/shard_map/quw,ugw->qgw/dot_general | solution.py:37
  97.1 2.6 %pad_maximum_fusion = bf16[2,256,1024]{1,0,2:T(2,128)(2,1)S(1)} fusion(bf16[2,256,512]{1,0,2:T(2,128)(2,1)} %fusion.4, bf16[2,256,512]{1,0,2:T(2,128)(2,1)} %fusion.5), kind=kLoop, calls=%fused_computation.21 | loop fusion | flops 524288 | bytes 2097152 | tf_op jit(solution)/shard_map/concatenate | solution.py:45
  99.6 1.5 %copy.24 = bf16[2,256,1024]{2,1,0:T(8,128)(2,1)S(1)} copy(bf16[2,256,1024]{1,0,2:T(2,128)(2,1)S(1)} %pad_maximum_fusion) | data formatting | bytes 2097152 | tf_op jit(solution)/shard_map/concatenate | solution.py:45
  101.1 0.1 copy.30
  101.2 1.6 %copy.36 = bf16[2,8,32,1024]{3,1,2,0:T(8,128)(2,1)} copy(bf16[2,8,32,1024]{3,2,1,0:T(8,128)(2,1)S(1)} %bitcast.61) | data formatting | bytes 2097152
  102.8 0.0 reduce-scatter.5.cloned.1.call-update
  102.8 1.9 %sort.17 = (s32[16]{0:T(128)}, s32[16]{0:T(128)S(1)}) sort(s32[16]{0:T(128)} %param.7, s32[16]{0:T(128)S(1)} %iota.50), dimensions={0}, to_apply=%region_0.1 | sort | flops 64 | bytes 256 | tf_op jit(solution)/shard_map/jit(argsort)/sort | solution.py:68
  104.7 0.1 broadcast_in_dim.68
  104.8 4.0 %multiply_convert_fusion = bf16[512,512]{1,0:T(8,128)(2,1)S(1)} fusion(f32[512]{0:T(512)S(1)} %select_multiply_fusion), kind=kLoop, calls=%fused_computation.27 | loop fusion | flops 4194304 | bytes 526336 | tf_op jit(solution)/shard_map/convert
  108.8 13.1 %reduce-scatter.5.cloned.1.call-done = bf16[8,32768]{1,0:T(8,128)(2,1)} async-done(((bf16[16,32768]{1,0:T(8,128)(2,1)}), bf16[8,32768]{1,0:T(8,128)(2,1)}) %reduce-scatter.5.cloned.1.call-update) | async-done | bytes 524304
  121.9 1.3 copy.37
  123.2 1.5 %fusion.12 = f32[2,8,16,512]{3,1,2,0:T(8,128)S(1)} fusion(bf16[512,512]{1,0:T(8,128)(2,1)} %get-tuple-element.10, bf16[512,512]{1,0:T(8,128)(2,1)S(1)} %multiply_convert_fusion, bf16[2,8,16,1024]{3,2,0,1:T(8,128)(2,1)S(1)} %bitcast.64), kind=kOutput, calls=%fused_computation.23 | convolution fusion | flops 270532608 | bytes 2097152 | tf_op jit(solution)/shard_map/dot_general | solution.py:90
  124.8 0.6 gather_fusion
  125.3 0.3 copy.26
  125.7 0.0 copy-done.5
  125.7 2.0 %fusion.23 = f32[2,128,512]{2,1,0:T(8,128)} fusion(f32[2,128,512]{2,1,0:T(8,128)} %param.5, f32[2,8,16,512]{3,2,1,0:T(8,128)S(1)} %copy.26, f32[2]{0:T(128)S(1)} %copy-done.5, pred[128]{0:T(512)(128)(4,1)S(1)} %broadcast_in_dim.68), kind=kLoop, calls=%fused_computation.38 | loop fusion | flops 393216 | bytes 1573000 | tf_op jit(solution)/shard_map/sub | solution.py:96
  (10 shorter events, 0.1 us)
Async XLA Ops:
  6.5 56.2 %all-gather.2.cloned.1.call-start = ((), (), s32[]{:S(2)}) async-start(), calls=%async_computation.1 | async-start | bytes 4456448 | tf_op jit(solution)/shard_map/all_gather | solution.py:75
  7.3 114.6 %reduce-scatter.5.cloned.1.call-start = ((), (), s32[]{:S(2)}) async-start(), calls=%async_computation.2 | async-start | bytes 1572864
  18.8 68.1 %copy-start.3 = (bf16[2,32,512]{1,0,2:T(2,128)(2,1)}, bf16[2,32,512]{1,0,2:T(2,128)(2,1)S(1)}, u32[]{:S(2)}) copy-start(bf16[2,32,512]{1,0,2:T(2,128)(2,1)S(1)} %copy.34) | copy-start | bytes 196612
  86.9 2.2 %copy-start.4 = (bf16[2,32,512]{1,0,2:T(2,128)(2,1)S(1)}, bf16[2,32,512]{1,0,2:T(2,128)(2,1)}, u32[]{:S(2)}) copy-start(bf16[2,32,512]{1,0,2:T(2,128)(2,1)} %copy.33) | copy-start | bytes 196612
  89.2 2.2 %copy-start = (f32[512]{0:T(512)S(1)}, f32[512]{0:T(512)}, u32[]{:S(2)}) copy-start(f32[512]{0:T(512)} %fusion.36) | copy-start | bytes 6148
  89.2 2.2 %copy-start.2 = (f32[512,256,2]{1,2,0:T(2,128)S(1)}, f32[512,256,2]{1,2,0:T(2,128)}, u32[]{:S(2)}) copy-start(f32[512,256,2]{1,2,0:T(2,128)} %fusion.41) | copy-start | bytes 3145732
  91.4 2.0 %copy-start.1 = (f32[512]{0:T(512)S(1)}, f32[512]{0:T(512)}, u32[]{:S(2)}) copy-start(f32[512]{0:T(512)} %broadcast_subtract_fusion) | copy-start | bytes 6148
  93.4 32.2 %copy-start.5 = (f32[2]{0:T(128)S(1)}, f32[2]{0:T(128)}, u32[]{:S(2)}) copy-start(f32[2]{0:T(128)} %param.9) | copy-start | bytes 28
Sparse Core Ops, SparseCore 0:
  9.5 53.2 all-gather.1
  102.9 18.9 reduce-scatter.4
where the time goes:
time: 135 us
  waiting for transfers between devices  55.7 us (41%)
  local copies, waits for them, and re-layouts  22.6 us (17%)
  matrix products  21.4 us (16%)
  other arithmetic  21.3 us (16%)
  between operations  13.6 us (10%)
    all_gather x1, waiting for transfers between devices, on_device(): piece_rows = lax.all_gather(primaries, 'shot', axis=2, tiled=True)  41.9 us
    unnamed x18, local copies, waits for them, and re-layouts  14.5 us
    unnamed x3, waiting for transfers between devices  13.8 us
    another operation x3, other arithmetic  13 us
    dot_general x4, matrix products, contract(): jnp.einsum('quw,ugw->qgw', leading_factor, trailing_factor, preferred_ele...  10.1 us
    dot_general x1, matrix products, on_device(): jnp.dot(piece_rows.reshape(-1, tap_count), forward[:tap_count], preferred...  8.11 us
    all_gather x1, local copies, waits for them, and re-layouts, on_device(): piece_rows = lax.all_gather(primaries, 'shot', axis=2, tiled=True)  5.61 us
  transfers between devices with their start and end apart: 2, of which 2 were waited for; matrix products, arithmetic and copies ran while one was open for 14% of the time, Pallas kernels for 0%

commit v1 on v0

v1 whole, which is shorter than its diff:
```python
import functools
import math

import jax
import jax.numpy as jnp
import ml_dtypes
import numpy as np
from jax import lax
from jax.experimental import pallas as pl
from jax.experimental.pallas import tpu as pltpu
from jax.sharding import PartitionSpec as P

MESH = pl.DeviceIdType.MESH
F32 = jnp.float32
BF16 = jnp.bfloat16


def fourier_matrices(samples):
    length = 2 * samples
    index = np.arange(samples)
    angles = (index[:, None] * index[None, :] % length) * (2.0 * math.pi / length)
    cosine, sine = np.cos(angles), np.sin(angles)
    alternate = 1.0 - 2.0 * (index % 2)
    forward_imag = -sine
    forward_imag[:, 0] = alternate
    forward = np.concatenate([cosine, forward_imag], axis=1)
    weights = np.where(index == 0, 1.0, 2.0) / length
    weights = np.concatenate([weights, weights])
    inverse = forward.T * weights[:, None]
    return forward.astype(ml_dtypes.bfloat16), inverse.astype(ml_dtypes.bfloat16)


def chip_at(place, chips):
    half = chips // 2
    side = place // half
    return 2 * (place + side * (chips - 1 - 2 * place)) + side


def kernel(
    sizes,
    plan_ref, scale_ref, where_ref, positions_ref, data_ref, primaries_ref, forward_ref, inverse_ref,
    out_ref,
    gathered, partner, e1, e2, e3, dr, di, dsum, spectrum, leaving, arrived,
    panel_sems, ring_send, ring_recv, leave_send, leave_recv,
):
    chips, surfs, shots, depth, width, samples, taps = sizes
    per_surf = width // surfs
    panels = 2 * chips
    shot = lax.axis_index("shot")
    surf = lax.axis_index("surf")
    chip, core = shot // 2, shot % 2
    height, side = chip // 2, chip % 2
    place = height + side * (chips - 1 - 2 * height)
    right = chip_at((place + 1) % chips, chips) * 2 + core
    left = chip_at((place + chips - 1) % chips, chips) * 2 + core

    barrier = pltpu.get_barrier_semaphore()
    pl.semaphore_signal(barrier, inc=1, device_id=(chip * 2 + 1 - core, surf), device_id_type=MESH)

    def greet(n, carry):
        other = (n // surfs) * 2 + core
        to = n % surfs

        @pl.when(n != chip * surfs + surf)
        def _():
            pl.semaphore_signal(barrier, inc=1, device_id=(other, to), device_id_type=MESH)

        return carry

    lax.fori_loop(0, chips * surfs, greet, 0)

    local = positions_ref[...] - surf * depth
    onehot = jnp.where(
        lax.broadcasted_iota(jnp.int32, (depth, local.shape[1]), 0) == local, 1.0, 0.0
    ).astype(BF16)
    for s in range(shots):
        value = data_ref[s]
        top = value.astype(BF16)
        rest = value - top.astype(F32)
        middle = rest.astype(BF16)
        low = (rest - middle.astype(F32)).astype(BF16)
        total = (
            jnp.dot(onehot, top, preferred_element_type=F32)
            + jnp.dot(onehot, middle, preferred_element_type=F32)
            + jnp.dot(onehot, low, preferred_element_type=F32)
        )
        gathered[place, s * depth:(s + 1) * depth, :] = total.astype(BF16)

    pl.semaphore_wait(barrier, chips * surfs)

    def ring_copy(direction, hops):
        if direction == 0:
            slot, to = (place + chips - hops) % chips, right
        else:
            slot, to = (place + hops) % chips, left
        return pltpu.make_async_remote_copy(
            src_ref=gathered.at[slot],
            dst_ref=gathered.at[slot],
            send_sem=ring_send.at[direction, hops],
            recv_sem=ring_recv.at[slot],
            device_id=(to, surf),
            device_id_type=MESH,
        )

    right_hops, left_hops = chips // 2, (chips - 1) // 2
    ring_copy(0, 0).start()
    ring_copy(1, 0).start()
    panel_copy = pltpu.make_async_remote_copy(
        src_ref=primaries_ref,
        dst_ref=partner,
        send_sem=panel_sems.at[0],
        recv_sem=panel_sems.at[1],
        device_id=(chip * 2 + 1 - core, surf),
        device_id_type=MESH,
    )
    panel_copy.start()

    block = 8

    def panel_spectra(source, which):
        def step(n, carry):
            rows = source[pl.ds(pl.multiple_of(n * block * width, block * width), block * width), :]
            value = jnp.dot(rows, forward_ref[:taps, :], preferred_element_type=F32)
            real, imag = value[:, :samples], value[:, samples:]
            first = lax.broadcasted_iota(jnp.int32, real.shape, 1) == 0
            shape = (block, width, samples)
            at = pl.ds(n * block, block)
            e1[at, which] = jnp.where(first, 0.0, real).reshape(shape)
            e2[at, which] = jnp.where(first, real, imag - real).reshape(shape)
            e3[at, which] = jnp.where(first, imag, imag + real).reshape(shape)
            return carry

        lax.fori_loop(0, depth // block, step, 0)

    panel_spectra(primaries_ref, 0)
    panel_copy.wait_recv()
    panel_spectra(partner, 1)

    def leave_copy(slot, to):
        return pltpu.make_async_remote_copy(
            src_ref=leaving.at[slot, to],
            dst_ref=arrived.at[place, surf],
            send_sem=leave_send.at[slot, to],
            recv_sem=leave_recv.at[place, surf],
            device_id=(chip_at(slot, chips) * 2 + core, to),
            device_id_type=MESH,
        )

    def one_chunk(e, carry):
        hops = (e + 1) // 2

        @pl.when(e % 2 == 1)
        def _():
            pltpu.make_async_copy(
                gathered.at[place], gathered.at[place], ring_recv.at[(place + chips - hops) % chips]
            ).wait()

            @pl.when(hops < right_hops)
            def _():
                ring_copy(0, hops).start()

            @pl.when(hops <= left_hops)
            def _():
                pltpu.make_async_copy(
                    gathered.at[place], gathered.at[place], ring_recv.at[(place + hops) % chips]
                ).wait()

            @pl.when(hops < left_hops)
            def _():
                ring_copy(1, hops).start()

        slot = (place + chips + (1 - 2 * (e % 2)) * hops) % chips
        value = jnp.dot(gathered[slot], forward_ref[...], preferred_element_type=F32)
        real, imag = value[:, :samples], value[:, samples:]
        dr[...] = real
        di[...] = imag
        dsum[...] = real + imag

        def one_tile(f, inner):
            lanes = pl.ds(pl.multiple_of(f * 128, 128), 128)
            zero = jnp.zeros((2 * width, 128), F32)
            k1, k2, k3 = [zero] * shots, [zero] * shots, [zero] * shots
            for x in range(depth):
                a1 = e1[x, :, :, lanes].reshape(2 * width, 128)
                a2 = e2[x, :, :, lanes].reshape(2 * width, 128)
                a3 = e3[x, :, :, lanes].reshape(2 * width, 128)
                for s in range(shots):
                    row = pl.ds(s * depth + x, 1)
                    k1[s] = k1[s] + a1 * dsum[row, lanes]
                    k2[s] = k2[s] + a2 * dr[row, lanes]
                    k3[s] = k3[s] + a3 * di[row, lanes]
            first = lax.broadcasted_iota(jnp.int32, (2 * width, 128), 1) + f * 128 == 0
            imag_lanes = pl.ds(pl.multiple_of(samples + f * 128, 128), 128)
            for s in range(shots):
                re = jnp.where(first, k2[s], k1[s] - k3[s])
                im = jnp.where(first, k3[s], k1[s] + k2[s])
                for h in range(surfs):
                    for b in range(2):
                        low = ((h * shots + s) * 2 + b) * per_surf
                        src = b * width + h * per_surf
                        spectrum[low:low + per_surf, lanes] = re[src:src + per_surf]
                        spectrum[low:low + per_surf, imag_lanes] = im[src:src + per_surf]
            return inner

        lax.fori_loop(0, samples // 128, one_tile, 0)
        back = jnp.dot(spectrum[...].astype(BF16), inverse_ref[...], preferred_element_type=F32)
        rows = shots * 2 * per_surf
        for h in range(surfs):
            piece = back[h * rows:(h + 1) * rows].astype(BF16)
            mine = jnp.logical_and(slot == place, surf == h)

            @pl.when(mine)
            def _():
                arrived[place, surf] = piece

            @pl.when(jnp.logical_not(mine))
            def _():
                leaving[slot, h] = piece
                leave_copy(slot, h).start()

        return carry

    lax.fori_loop(0, chips, one_chunk, 0)

    first_panel, swap, base = where_ref[0:1, :], where_ref[1:2, :], where_ref[2:3, :]
    panel = first_panel + swap + core - 2 * core * swap
    target = base
    for n in range(panels):
        target = target + jnp.where(panel == n, plan_ref[n], 0)
    rows_out = data_ref.shape[0] * data_ref.shape[1]
    place_rows = jnp.where(
        lax.broadcasted_iota(jnp.int32, (rows_out, target.shape[1]), 0) == target, 1.0, 0.0
    ).astype(BF16)

    def settle(n, carry):
        slot, other = n // surfs, n % surfs

        @pl.when(n != place * surfs + surf)
        def _():
            leave_copy(slot, other).wait_send()
            pltpu.make_async_copy(
                arrived.at[slot, other], arrived.at[slot, other], leave_recv.at[slot, other]
            ).wait()

        return carry

    lax.fori_loop(0, chips * surfs, settle, 0)
    moved = arrived[...].reshape(target.shape[1], samples)
    prediction = jnp.dot(place_rows, moved, preferred_element_type=F32)
    receivers = data_ref.shape[1]
    for s in range(shots):
        out_ref[s] = data_ref[s] - scale_ref[s] * prediction[s * receivers:(s + 1) * receivers]

    for hops in range(right_hops):
        ring_copy(0, hops).wait_send()
    for hops in range(left_hops):
        ring_copy(1, hops).wait_send()
    panel_copy.wait_send()


def on_device(chips, surfs, data, positions, plan, primaries, scale):
    shots, receivers, samples = data.shape
    depth, width, _, taps = primaries.shape
    per_surf = width // surfs
    forward, inverse = fourier_matrices(samples)
    rows = shots * 2 * per_surf
    order = [
        (2 * chip_at(c, chips), b, (s * per_surf + q) * 2 * chips)
        for c in range(chips)
        for _ in range(surfs)
        for s in range(shots)
        for b in range(2)
        for q in range(per_surf)
    ]
    where_rows = np.zeros((8, len(order)), np.int32)
    where_rows[:3] = np.array(order, np.int32).T
    vmem = pl.BlockSpec(memory_space=pltpu.VMEM)
    smem = pl.BlockSpec(memory_space=pltpu.SMEM)
    sizes = (chips, surfs, shots, depth, width, samples, taps)
    return pl.pallas_call(
        functools.partial(kernel, sizes),
        out_shape=jax.ShapeDtypeStruct(data.shape, data.dtype),
        in_specs=[smem, smem] + [vmem] * 6,
        out_specs=vmem,
        scratch_shapes=[
            pltpu.VMEM((chips, shots * depth, samples), BF16),
            pltpu.VMEM((depth * width, taps), BF16),
            pltpu.VMEM((depth, 2, width, samples), F32),
            pltpu.VMEM((depth, 2, width, samples), F32),
            pltpu.VMEM((depth, 2, width, samples), F32),
            pltpu.VMEM((shots * depth, samples), F32),
            pltpu.VMEM((shots * depth, samples), F32),
            pltpu.VMEM((shots * depth, samples), F32),
            pltpu.VMEM((surfs * rows, 2 * samples), F32),
            pltpu.VMEM((chips, surfs, rows, samples), BF16),
            pltpu.VMEM((chips, surfs, rows, samples), BF16),
            pltpu.SemaphoreType.DMA((2,)),
            pltpu.SemaphoreType.DMA((2, chips)),
            pltpu.SemaphoreType.DMA((chips,)),
            pltpu.SemaphoreType.DMA((chips, surfs)),
            pltpu.SemaphoreType.DMA((chips, surfs)),
        ],
        compiler_params=pltpu.CompilerParams(collective_id=0, has_side_effects=True),
        name="predict",
    )(
        plan,
        scale,
        jnp.asarray(where_rows),
        positions.reshape(1, receivers),
        data,
        primaries.reshape(depth * width, taps),
        jnp.asarray(forward),
        jnp.asarray(inverse),
    )


def solution(mesh):
    chips, surfs = mesh.shape["shot"] // 2, mesh.shape["surf"]
    in_specs = (P("shot", "surf", None), P("surf"), P(), P("surf", None, "shot", None), P("shot"))
    out_specs = P("shot", "surf", None)
    return jax.shard_map(
        functools.partial(on_device, chips, surfs),
        mesh=mesh, in_specs=in_specs, out_specs=out_specs, check_vma=False,
    )
```

time: 135 us -> 37.5 us (0.28)
  waiting for transfers between devices: 55.7 us -> 0 us
  Pallas kernels: 0 us -> 34.9 us
  matrix products: 21.4 us -> 0 us
  other arithmetic: 21.3 us -> 0 us
  local copies, waits for them, and re-layouts: 22.6 us -> 1.87 us
  between operations: 13.6 us -> 0.01 us
    all_gather x1 -> x0, waiting for transfers between devices: 41.9 us -> none  [on_device(): piece_rows = lax.all_gather(primaries, 'shot', axis=2, tiled=True)]
    pallas_call x0 -> x1, Pallas kernels: none -> 34.9 us  [on_device(): pl.pallas_call(functools.partial(kernel, sizes), out_shape=jax.ShapeDtype...]
    dot_general x8 -> x0, matrix products: 21.4 us -> none  [the longest x4 10.1 us: contract(): jnp.einsum('quw,ugw->qgw', leading_factor, trailing_factor, preferred_ele...]
    unnamed x3 -> x0, waiting for transfers between devices: 13.8 us -> none
    another operation x3 -> x0, other arithmetic: 13 us -> none
    unnamed x18 -> x1, local copies, waits for them, and re-layouts: 14.5 us -> 1.87 us
    all_gather x1 -> x0, local copies, waits for them, and re-layouts: 5.61 us -> none  [on_device(): piece_rows = lax.all_gather(primaries, 'shot', axis=2, tiled=True)]
    sub x3 -> x0, other arithmetic: 3.25 us -> none  [the longest x1 2 us: on_device(): return data - scale[:, None, None] * prediction]
  transfers between devices with their start and end apart: 2 -> 0, of which waited for: 2 -> 0; matrix products, arithmetic and copies ran while one was open for 14% -> 0% of each run, Pallas kernels for 0% -> 0%
where the time goes in v1:
time: 37.5 us; the launch traced here: 36.8 us
  Pallas kernels  34.9 us (93%)
  local copies, waits for them, and re-layouts  1.87 us (5%)
    pallas_call x1, Pallas kernels, on_device(): pl.pallas_call(functools.partial(kernel, sizes), out_shape=jax.ShapeDtype...  34.9 us
    unnamed x1, local copies, waits for them, and re-layouts  1.87 us

profile of v1, /device:TPU:0, one launch (start us, length us, event | category | flops | bytes accessed | tf_op | source)
XLA Modules:
  0.0 36.8 jit_solution(16997393152405728669)
XLA Ops:
  0.0 34.9 %predict.1 = f32[2,128,512]{2,1,0:T(8,128)} custom-call(s32[16]{0:T(128)} %plan_ref.1, f32[2]{0:T(128)} %scale_ref.1, s32[8,512]{1,0:T(8,128)} %constant.6.clone.where_ref, s32[1,128]{1,0:T(1,128)} %bitcast.3, f32[2,128,512]{2,1,0:T(8,128)} %data_ref.1, bf16[512,256]{1,0:T(8,128)(2,1)} %bitcast.2, bf16[512,1024]{1,0:T(8,128)(2,1)} %constant.7.clone.forward_ref, ...), custom_call_target="tpu_custom_call" | custom-call | tf_op jit(solution)/shard_map/predict/pallas_call | solution.py:280
  34.9 1.9 %copy.10 = f32[2,128,512]{2,1,0:T(8,128)} copy(f32[2,128,512]{2,1,0:T(8,128)} %predict.1) | data formatting | bytes 1048576

commit v2 on v1

--- a/solution.py
+++ b/solution.py
@@ -13,6 +13,7 @@
 MESH = pl.DeviceIdType.MESH
 F32 = jnp.float32
 BF16 = jnp.bfloat16
+UNROLL = 8
 
 
 def fourier_matrices(samples):
@@ -40,7 +41,7 @@
     sizes,
     plan_ref, scale_ref, where_ref, positions_ref, data_ref, primaries_ref, forward_ref, inverse_ref,
     out_ref,
-    gathered, partner, e1, e2, e3, dr, di, dsum, spectrum, leaving, arrived,
+    gathered, partner, e1, e2, e3, factors, spectrum, leaving, arrived,
     panel_sems, ring_send, ring_recv, leave_send, leave_recv,
 ):
     chips, surfs, shots, depth, width, samples, taps = sizes
@@ -123,11 +124,16 @@
             value = jnp.dot(rows, forward_ref[:taps, :], preferred_element_type=F32)
             real, imag = value[:, :samples], value[:, samples:]
             first = lax.broadcasted_iota(jnp.int32, real.shape, 1) == 0
-            shape = (block, width, samples)
+            shape = (block, width, 128)
             at = pl.ds(n * block, block)
-            e1[at, which] = jnp.where(first, 0.0, real).reshape(shape)
-            e2[at, which] = jnp.where(first, real, imag - real).reshape(shape)
-            e3[at, which] = jnp.where(first, imag, imag + real).reshape(shape)
+            values = (
+                jnp.where(first, 0.0, real),
+                jnp.where(first, real, imag - real),
+                jnp.where(first, imag, imag + real),
+            )
+            for ref, value in zip((e1, e2, e3), values):
+                for f in range(samples // 128):
+                    ref[f, at, which] = value[:, f * 128:(f + 1) * 128].reshape(shape)
             return carry
 
         lax.fori_loop(0, depth // block, step, 0)
@@ -172,23 +178,51 @@
         slot = (place + chips + (1 - 2 * (e % 2)) * hops) % chips
         value = jnp.dot(gathered[slot], forward_ref[...], preferred_element_type=F32)
         real, imag = value[:, :samples], value[:, samples:]
-        dr[...] = real
-        di[...] = imag
-        dsum[...] = real + imag
+        for k, part in enumerate((real + imag, real, imag)):
+            for s in range(shots):
+                for f in range(samples // 128):
+                    factors[f, s * 3 + k, :depth, :] = part[
+                        s * depth:(s + 1) * depth, f * 128:(f + 1) * 128
+                    ]
 
         def one_tile(f, inner):
             lanes = pl.ds(pl.multiple_of(f * 128, 128), 128)
-            zero = jnp.zeros((2 * width, 128), F32)
-            k1, k2, k3 = [zero] * shots, [zero] * shots, [zero] * shots
-            for x in range(depth):
-                a1 = e1[x, :, :, lanes].reshape(2 * width, 128)
-                a2 = e2[x, :, :, lanes].reshape(2 * width, 128)
-                a3 = e3[x, :, :, lanes].reshape(2 * width, 128)
-                for s in range(shots):
-                    row = pl.ds(s * depth + x, 1)
-                    k1[s] = k1[s] + a1 * dsum[row, lanes]
-                    k2[s] = k2[s] + a2 * dr[row, lanes]
-                    k3[s] = k3[s] + a3 * di[row, lanes]
+            tiles = 2 * width // 8
+
+            def positions(n, sums):
+                sums = list(sums)
+                for j in range(UNROLL):
+                    x = n * UNROLL + j
+                    rows = [
+                        [
+                            jnp.broadcast_to(
+                                factors.at[f, s * 3 + k, pl.ds(pl.multiple_of(n * UNROLL, UNROLL), UNROLL)][j:j + 1],
+                                (8, 128),
+                            )
+                            for k in range(3)
+                        ]
+                        for s in range(shots)
+                    ]
+                    for t in range(tiles):
+                        b, q = t * 8 // width, t * 8 % width
+                        for k, ref in enumerate((e1, e2, e3)):
+                            factor = ref[f, x, b, q:q + 8]
+                            for s in range(shots):
+                                at = (s * 3 + k) * tiles + t
+                                sums[at] = sums[at] + factor * rows[s][k]
+                return tuple(sums)
+
+            zero = jnp.zeros((8, 128), F32)
+            sums = lax.fori_loop(
+                0, depth // UNROLL, positions, (zero,) * (3 * shots * tiles)
+            )
+            k1, k2, k3 = [
+                [
+                    jnp.concatenate(sums[(s * 3 + k) * tiles:(s * 3 + k + 1) * tiles], axis=0)
+                    for s in range(shots)
+                ]
+                for k in range(3)
+            ]
             first = lax.broadcasted_iota(jnp.int32, (2 * width, 128), 1) + f * 128 == 0
             imag_lanes = pl.ds(pl.multiple_of(samples + f * 128, 128), 128)
             for s in range(shots):
@@ -285,12 +319,10 @@
         scratch_shapes=[
             pltpu.VMEM((chips, shots * depth, samples), BF16),
             pltpu.VMEM((depth * width, taps), BF16),
-            pltpu.VMEM((depth, 2, width, samples), F32),
-            pltpu.VMEM((depth, 2, width, samples), F32),
-            pltpu.VMEM((depth, 2, width, samples), F32),
-            pltpu.VMEM((shots * depth, samples), F32),
-            pltpu.VMEM((shots * depth, samples), F32),
-            pltpu.VMEM((shots * depth, samples), F32),
+            pltpu.VMEM((samples // 128, depth, 2, width, 128), F32),
+            pltpu.VMEM((samples // 128, depth, 2, width, 128), F32),
+            pltpu.VMEM((samples // 128, depth, 2, width, 128), F32),
+            pltpu.VMEM((samples // 128, shots * 3, depth + 8, 128), F32),
             pltpu.VMEM((surfs * rows, 2 * samples), F32),
             pltpu.VMEM((chips, surfs, rows, samples), BF16),
             pltpu.VMEM((chips, surfs, rows, samples), BF16),

time: 37.5 us -> 35.9 us (0.957)
  the two profiles are of different devices: /device:TPU:0 before, /device:TPU:16 now
where the time goes in v2:
time: 35.9 us; the launch traced here: 35.7 us
  Pallas kernels  33.8 us (94%)
  local copies, waits for them, and re-layouts  1.87 us (5%)
    pallas_call x1, Pallas kernels, on_device(): pl.pallas_call(functools.partial(kernel, sizes), out_shape=jax.ShapeDtype...  33.8 us
    unnamed x1, local copies, waits for them, and re-layouts  1.87 us

profile of v2, /device:TPU:16, one launch (start us, length us, event | category | flops | bytes accessed | tf_op | source)
XLA Modules:
  0.0 35.7 jit_solution(449392896195572882)
XLA Ops:
  0.0 33.8 %predict.1 = f32[2,128,512]{2,1,0:T(8,128)} custom-call(s32[16]{0:T(128)} %plan_ref.1, f32[2]{0:T(128)} %scale_ref.1, s32[8,512]{1,0:T(8,128)} %constant.6.clone.where_ref, s32[1,128]{1,0:T(1,128)} %bitcast.3, f32[2,128,512]{2,1,0:T(8,128)} %data_ref.1, bf16[512,256]{1,0:T(8,128)(2,1)} %bitcast.2, bf16[512,1024]{1,0:T(8,128)(2,1)} %constant.7.clone.forward_ref, ...), custom_call_target="tpu_custom_call" | custom-call | tf_op jit(solution)/shard_map/predict/pallas_call | solution.py:314
  33.8 1.9 %copy.10 = f32[2,128,512]{2,1,0:T(8,128)} copy(f32[2,128,512]{2,1,0:T(8,128)} %predict.1) | data formatting | bytes 1048576

commit v3 on v2

--- a/solution.py
+++ b/solution.py
@@ -13,7 +13,7 @@
 MESH = pl.DeviceIdType.MESH
 F32 = jnp.float32
 BF16 = jnp.bfloat16
-UNROLL = 8
+UNROLL = 16
 
 
 def fourier_matrices(samples):
@@ -39,10 +39,11 @@
 
 def kernel(
     sizes,
-    plan_ref, scale_ref, where_ref, positions_ref, data_ref, primaries_ref, forward_ref, inverse_ref,
+    plan_ref, scale_ref, where_ref, positions_ref, data_ref, primaries_ref, forward_hbm, inverse_hbm,
     out_ref,
-    gathered, partner, e1, e2, e3, factors, spectrum, leaving, arrived,
-    panel_sems, ring_send, ring_recv, leave_send, leave_recv,
+    forward_ref, inverse_ref, gathered, partner, e1, e2, e3, factors, spectrum,
+    crossing, crossed, leaving, arrived,
+    load_sems, panel_sems, ring_send, ring_recv, cross_send, cross_recv, leave_send, leave_recv,
 ):
     chips, surfs, shots, depth, width, samples, taps = sizes
     per_surf = width // surfs
@@ -58,17 +59,18 @@
     barrier = pltpu.get_barrier_semaphore()
     pl.semaphore_signal(barrier, inc=1, device_id=(chip * 2 + 1 - core, surf), device_id_type=MESH)
 
-    def greet(n, carry):
-        other = (n // surfs) * 2 + core
-        to = n % surfs
-
-        @pl.when(n != chip * surfs + surf)
+    for to in (right, left):
+        pl.semaphore_signal(barrier, inc=1, device_id=(to, surf), device_id_type=MESH)
+    for h in range(surfs):
+
+        @pl.when(h != surf)
         def _():
-            pl.semaphore_signal(barrier, inc=1, device_id=(other, to), device_id_type=MESH)
-
-        return carry
-
-    lax.fori_loop(0, chips * surfs, greet, 0)
+            pl.semaphore_signal(barrier, inc=1, device_id=(shot, h), device_id_type=MESH)
+
+    load_forward = pltpu.make_async_copy(forward_hbm, forward_ref, load_sems.at[0])
+    load_inverse = pltpu.make_async_copy(inverse_hbm, inverse_ref, load_sems.at[1])
+    load_forward.start()
+    load_inverse.start()
 
     local = positions_ref[...] - surf * depth
     onehot = jnp.where(
@@ -87,7 +89,7 @@
         )
         gathered[place, s * depth:(s + 1) * depth, :] = total.astype(BF16)
 
-    pl.semaphore_wait(barrier, chips * surfs)
+    pl.semaphore_wait(barrier, surfs + 2)
 
     def ring_copy(direction, hops):
         if direction == 0:
@@ -138,24 +140,54 @@
 
         lax.fori_loop(0, depth // block, step, 0)
 
+    load_forward.wait()
     panel_spectra(primaries_ref, 0)
     panel_copy.wait_recv()
     panel_spectra(partner, 1)
-
-    def leave_copy(slot, to):
+    load_inverse.wait()
+
+    def cross_copy(e, to):
         return pltpu.make_async_remote_copy(
-            src_ref=leaving.at[slot, to],
-            dst_ref=arrived.at[place, surf],
-            send_sem=leave_send.at[slot, to],
-            recv_sem=leave_recv.at[place, surf],
-            device_id=(chip_at(slot, chips) * 2 + core, to),
+            src_ref=crossing.at[e, to],
+            dst_ref=crossed.at[e, surf],
+            send_sem=cross_send.at[e, to],
+            recv_sem=cross_recv.at[e, surf],
+            device_id=(shot, to),
             device_id_type=MESH,
         )
 
+    def leave_copy(slot):
+        return pltpu.make_async_remote_copy(
+            src_ref=leaving.at[slot],
+            dst_ref=arrived.at[place],
+            send_sem=leave_send.at[slot],
+            recv_sem=leave_recv.at[place],
+            device_id=(chip_at(slot, chips) * 2 + core, surf),
+            device_id_type=MESH,
+        )
+
+    def slot_of(e):
+        turn = (e + 1) % chips
+        hops = (turn + 1) // 2
+        return (place + chips + (1 - 2 * (turn % 2)) * hops) % chips
+
+    def combined(e):
+        for h in range(surfs):
+
+            @pl.when(h != surf)
+            def _():
+                pltpu.make_async_copy(crossed.at[e, h], crossed.at[e, h], cross_recv.at[e, h]).wait()
+
+        total = crossed[e, 0].astype(F32)
+        for h in range(1, surfs):
+            total = total + crossed[e, h].astype(F32)
+        return total.astype(BF16)
+
     def one_chunk(e, carry):
-        hops = (e + 1) // 2
-
-        @pl.when(e % 2 == 1)
+        turn = (e + 1) % chips
+        hops = (turn + 1) // 2
+
+        @pl.when(turn % 2 == 1)
         def _():
             pltpu.make_async_copy(
                 gathered.at[place], gathered.at[place], ring_recv.at[(place + chips - hops) % chips]
@@ -175,7 +207,7 @@
             def _():
                 ring_copy(1, hops).start()
 
-        slot = (place + chips + (1 - 2 * (e % 2)) * hops) % chips
+        slot = slot_of(e)
         value = jnp.dot(gathered[slot], forward_ref[...], preferred_element_type=F32)
         real, imag = value[:, :samples], value[:, samples:]
         for k, part in enumerate((real + imag, real, imag)):
@@ -241,20 +273,26 @@
         rows = shots * 2 * per_surf
         for h in range(surfs):
             piece = back[h * rows:(h + 1) * rows].astype(BF16)
-            mine = jnp.logical_and(slot == place, surf == h)
-
-            @pl.when(mine)
-            def _():
-                arrived[place, surf] = piece
-
-            @pl.when(jnp.logical_not(mine))
-            def _():
-                leaving[slot, h] = piece
-                leave_copy(slot, h).start()
+
+            @pl.when(surf == h)
+            def _():
+                crossed[e, h] = piece
+
+            @pl.when(surf != h)
+            def _():
+                crossing[e, h] = piece
+                cross_copy(e, h).start()
+
+        @pl.when(e > 0)
+        def _():
+            before = slot_of(e - 1)
+            leaving[before] = combined(e - 1)
+            leave_copy(before).start()
 
         return carry
 
     lax.fori_loop(0, chips, one_chunk, 0)
+    arrived[place] = combined(chips - 1)
 
     first_panel, swap, base = where_ref[0:1, :], where_ref[1:2, :], where_ref[2:3, :]
     panel = first_panel + swap + core - 2 * core * swap
@@ -267,18 +305,20 @@
     ).astype(BF16)
 
     def settle(n, carry):
-        slot, other = n // surfs, n % surfs
-
-        @pl.when(n != place * surfs + surf)
+        for h in range(surfs):
+
+            @pl.when(h != surf)
+            def _():
+                cross_copy(n, h).wait_send()
+
+        @pl.when(n != place)
         def _():
-            leave_copy(slot, other).wait_send()
-            pltpu.make_async_copy(
-                arrived.at[slot, other], arrived.at[slot, other], leave_recv.at[slot, other]
-            ).wait()
+            leave_copy(n).wait_send()
+            pltpu.make_async_copy(arrived.at[n], arrived.at[n], leave_recv.at[n]).wait()
 
         return carry
 
-    lax.fori_loop(0, chips * surfs, settle, 0)
+    lax.fori_loop(0, chips, settle, 0)
     moved = arrived[...].reshape(target.shape[1], samples)
     prediction = jnp.dot(place_rows, moved, preferred_element_type=F32)
     receivers = data_ref.shape[1]
@@ -301,7 +341,6 @@
     order = [
         (2 * chip_at(c, chips), b, (s * per_surf + q) * 2 * chips)
         for c in range(chips)
-        for _ in range(surfs)
         for s in range(shots)
         for b in range(2)
         for q in range(per_surf)
@@ -314,9 +353,11 @@
     return pl.pallas_call(
         functools.partial(kernel, sizes),
         out_shape=jax.ShapeDtypeStruct(data.shape, data.dtype),
-        in_specs=[smem, smem] + [vmem] * 6,
+        in_specs=[smem, smem] + [vmem] * 4 + [pl.BlockSpec(memory_space=pl.ANY)] * 2,
         out_specs=vmem,
         scratch_shapes=[
+            pltpu.VMEM(forward.shape, BF16),
+            pltpu.VMEM(inverse.shape, BF16),
             pltpu.VMEM((chips, shots * depth, samples), BF16),
             pltpu.VMEM((depth * width, taps), BF16),
             pltpu.VMEM((samples // 128, depth, 2, width, 128), F32),
@@ -326,11 +367,16 @@
             pltpu.VMEM((surfs * rows, 2 * samples), F32),
             pltpu.VMEM((chips, surfs, rows, samples), BF16),
             pltpu.VMEM((chips, surfs, rows, samples), BF16),
+            pltpu.VMEM((chips, rows, samples), BF16),
+            pltpu.VMEM((chips, rows, samples), BF16),
+            pltpu.SemaphoreType.DMA((2,)),
             pltpu.SemaphoreType.DMA((2,)),
             pltpu.SemaphoreType.DMA((2, chips)),
             pltpu.SemaphoreType.DMA((chips,)),
             pltpu.SemaphoreType.DMA((chips, surfs)),
             pltpu.SemaphoreType.DMA((chips, surfs)),
+            pltpu.SemaphoreType.DMA((chips,)),
+            pltpu.SemaphoreType.DMA((chips,)),
         ],
         compiler_params=pltpu.CompilerParams(collective_id=0, has_side_effects=True),
         name="predict",

time: 35.9 us -> 35.5 us (0.989)
  the two profiles are of different devices: /device:TPU:16 before, /device:TPU:0 now
where the time goes in v3:
time: 35.5 us; the launch traced here: 35.4 us
  Pallas kernels  33.5 us (94%)
  local copies, waits for them, and re-layouts  1.87 us (5%)
    pallas_call x1, Pallas kernels, on_device(): pl.pallas_call(functools.partial(kernel, sizes), out_shape=jax.ShapeDtype...  33.5 us
    unnamed x1, local copies, waits for them, and re-layouts  1.87 us

profile of v3, /device:TPU:0, one launch (start us, length us, event | category | flops | bytes accessed | tf_op | source)
XLA Modules:
  0.0 35.4 jit_solution(6601864647698254933)
XLA Ops:
  0.0 33.5 %predict.1 = f32[2,128,512]{2,1,0:T(8,128)} custom-call(s32[16]{0:T(128)} %plan_ref.1, f32[2]{0:T(128)} %scale_ref.1, s32[8,256]{1,0:T(8,128)} %constant.6.clone.where_ref, s32[1,128]{1,0:T(1,128)} %bitcast.3, f32[2,128,512]{2,1,0:T(8,128)} %data_ref.1, bf16[512,256]{1,0:T(8,128)(2,1)} %bitcast.2, bf16[512,1024]{1,0:T(8,128)(2,1)} %constant.7.clone.forward_hbm, ...), custom_call_target="tpu_custom_call" | custom-call | tf_op jit(solution)/shard_map/predict/pallas_call | solution.py:353
  33.5 1.9 %copy.10 = f32[2,128,512]{2,1,0:T(8,128)} copy(f32[2,128,512]{2,1,0:T(8,128)} %predict.1) | data formatting | bytes 1048576

commit v4 on v3

--- a/solution.py
+++ b/solution.py
@@ -14,6 +14,7 @@
 F32 = jnp.float32
 BF16 = jnp.bfloat16
 UNROLL = 16
+LAG = 2
 
 
 def fourier_matrices(samples):
@@ -182,6 +183,11 @@
         for h in range(1, surfs):
             total = total + crossed[e, h].astype(F32)
         return total.astype(BF16)
+
+    def pass_on(e):
+        slot = slot_of(e)
+        leaving[slot] = combined(e)
+        leave_copy(slot).start()
 
     def one_chunk(e, carry):
         turn = (e + 1) % chips
@@ -283,15 +289,15 @@
                 crossing[e, h] = piece
                 cross_copy(e, h).start()
 
-        @pl.when(e > 0)
+        @pl.when(e >= LAG)
         def _():
-            before = slot_of(e - 1)
-            leaving[before] = combined(e - 1)
-            leave_copy(before).start()
+            pass_on(e - LAG)
 
         return carry
 
     lax.fori_loop(0, chips, one_chunk, 0)
+    for e in range(chips - LAG, chips - 1):
+        pass_on(e)
     arrived[place] = combined(chips - 1)
 
     first_panel, swap, base = where_ref[0:1, :], where_ref[1:2, :], where_ref[2:3, :]

time: 35.5 us -> 32.4 us (0.913)
  Pallas kernels: 33.5 us -> 30.4 us
    pallas_call x1, Pallas kernels: 33.5 us -> 30.4 us  [on_device(): pl.pallas_call(functools.partial(kernel, sizes), out_shape=jax.ShapeDtype...]
where the time goes in v4:
time: 32.4 us; the launch traced here: 32.3 us
  Pallas kernels  30.4 us (94%)
  local copies, waits for them, and re-layouts  1.87 us (6%)
    pallas_call x1, Pallas kernels, on_device(): pl.pallas_call(functools.partial(kernel, sizes), out_shape=jax.ShapeDtype...  30.4 us
    unnamed x1, local copies, waits for them, and re-layouts  1.87 us

profile of v4, /device:TPU:0, one launch (start us, length us, event | category | flops | bytes accessed | tf_op | source)
XLA Modules:
  0.0 32.3 jit_solution(2766139434834389730)
XLA Ops:
  0.0 30.4 %predict.1 = f32[2,128,512]{2,1,0:T(8,128)} custom-call(s32[16]{0:T(128)} %plan_ref.1, f32[2]{0:T(128)} %scale_ref.1, s32[8,256]{1,0:T(8,128)} %constant.6.clone.where_ref, s32[1,128]{1,0:T(1,128)} %bitcast.3, f32[2,128,512]{2,1,0:T(8,128)} %data_ref.1, bf16[512,256]{1,0:T(8,128)(2,1)} %bitcast.2, bf16[512,1024]{1,0:T(8,128)(2,1)} %constant.7.clone.forward_hbm, ...), custom_call_target="tpu_custom_call" | custom-call | tf_op jit(solution)/shard_map/predict/pallas_call | solution.py:359
  30.4 1.9 %copy.10 = f32[2,128,512]{2,1,0:T(8,128)} copy(f32[2,128,512]{2,1,0:T(8,128)} %predict.1) | data formatting | bytes 1048576
